TPU v7x, 256 devices: a whole 4x4x8 slice. The times are simulated.
256 devices in a mesh: dp: 4 (over y), segment: 8 (over z_hi, x), chan: 8 (over z_lo, core).
Axes of the slice: x: 4, y: 4, z: 8 (z_hi: 2, z_lo: 4; z = z_hi * 4 + z_lo), core: 2. Of those that a mesh axis runs over, the one named last changes fastest.
Arguments:
- x_input: bfloat16 [4, 4, 256, 1024], P(None, 'dp', None, 'chan'), may hold values from -48 to 48
- d_output: bfloat16 [4, 4, 256, 1024], P(None, 'dp', None, 'chan'), may hold values from -6 to 6
- weights: bfloat16 [8, 9, 1024, 1024], P('segment', None, None, 'chan'), may hold values from -0.0625 to 0.0625
- gains: float32 [8, 1024], P('segment', 'chan'), may hold values from 0.5 to 1.5
- biases: float32 [8, 1024], P('segment', 'chan'), may hold values from -3 to 3
Outputs:
- d_weights: float32 [8, 9, 1024, 1024], P('segment', None, None, 'chan')
- d_gains: float32 [8, 1024], P('segment', 'chan')
- d_biases: float32 [8, 1024], P('segment', 'chan')
All inputs are finite; a program needn't handle non-finite values.
Results may differ from a plain program's by a relative error of at most 0.025.
Values may be sent and summed in bfloat16 or wider, within the bound.
No kernel may reach another device: no remote copies, remote signals or barrier semaphores. Data moves between devices by JAX's collectives and lax.ppermute only.
A program may use at most 64 MiB of HBM per device.

v0:
```python
import jax
import jax.numpy as jnp
from jax import lax
from jax.sharding import PartitionSpec as P

GROUPS = 32
SIDE = 16
EPSILON = 1e-05


def shifted(shard, axis, by):
    length = lax.axis_size(axis)
    pairs = [(i, i + by) for i in range(length) if 0 <= i + by < length]
    return lax.ppermute(shard, axis, pairs)


def expand_groups(statistic, group_width):
    return jnp.repeat(statistic, group_width, axis=1)[:, None, :]


def group_sums(values, group_width):
    batch_count, pixel_count, channels = values.shape
    grouped = values.reshape(batch_count, pixel_count, channels // group_width, group_width)
    return jnp.sum(grouped, axis=(1, 3))


def shifted_stack(images, forward_taps):
    batch_count, pixel_count, channels = images.shape
    square = images.reshape(batch_count, SIDE, SIDE, channels)
    padded = jnp.pad(square, ((0, 0), (1, 1), (1, 1), (0, 0)))
    tap_list = []
    for tap_y in range(3):
        for tap_x in range(3):
            start_y = tap_y if forward_taps else 2 - tap_y
            start_x = tap_x if forward_taps else 2 - tap_x
            window = padded[:, start_y : start_y + SIDE, start_x : start_x + SIDE, :]
            tap_list.append(window.reshape(batch_count * pixel_count, channels))
    return jnp.stack(tap_list)


def take_slot(buffer, slot_index):
    return lax.dynamic_index_in_dim(buffer, slot_index, 0, keepdims=False)


def put_slot(buffer, value, slot_index, allowed):
    current = take_slot(buffer, slot_index)
    return lax.dynamic_update_index_in_dim(
        buffer, jnp.where(allowed, value, current), slot_index, 0
    )


def local(x_input, d_output, weights, gains, biases):
    segments = lax.axis_size("segment")
    half_way = segments // 2
    position = lax.axis_index("segment")
    is_down = position < half_way
    level = jnp.where(is_down, position, 2 * half_way - 1 - position)
    weight = weights[0]
    gain_row = gains[0]
    bias_row = biases[0]
    micro_count, images, pixels, local_width = x_input.shape
    full_width = weight.shape[1]
    group_width = full_width // GROUPS
    local_groups = local_width // group_width
    row_count = images * pixels
    group_count = pixels * group_width
    tick_count = micro_count + segments - 1
    bwd_place = 2 * half_way - 1 - position
    act_shape = (images, pixels, local_width)
    below_slot = jnp.clip(position - 1, 0, half_way - 1)
    above_slot = jnp.clip(level + 1, 0, half_way - 1)
    has_above = level < half_way - 1
    before_slot = jnp.clip(level - 1, 0, half_way - 1)

    def normalize(values, group_mean, group_rstd):
        normed = (values - expand_groups(group_mean, group_width)) * expand_groups(
            group_rstd, group_width
        )
        return (normed, normed * gain_row + bias_row)

    def forward_tick(tick_index, loop_state):
        stack_recv, saved_inputs, saved_mean, saved_rstd, saved_full = loop_state
        micro_index = tick_index - position
        active = (micro_index >= 0) & (micro_index < micro_count)
        slot_index = jnp.clip(micro_index, 0, micro_count - 1)
        first_in = jnp.where(
            position == 0, take_slot(x_input, slot_index), take_slot(stack_recv, below_slot)
        )
        skip_part = take_slot(stack_recv, level).astype(jnp.float32)
        upper_part = jnp.where(
            has_above, take_slot(stack_recv, above_slot).astype(jnp.float32), 0.0
        )
        joined = (upper_part + skip_part).astype(jnp.bfloat16)
        inputs = jnp.where(is_down, first_in, joined)
        values = inputs.astype(jnp.float32)
        group_mean = group_sums(values, group_width) / group_count
        centred = values - expand_groups(group_mean, group_width)
        variance = group_sums(centred * centred, group_width) / group_count
        group_rstd = lax.rsqrt(variance + EPSILON)
        normed, pre_act = normalize(values, group_mean, group_rstd)
        hidden = (pre_act * jax.nn.sigmoid(pre_act)).astype(jnp.bfloat16)
        empty_sum = jnp.zeros((row_count, local_width), jnp.float32)
        shard_piece = lax.all_gather(hidden, "chan", axis=2, tiled=True)
        conv_out = lax.cond(
            active,
            lambda: empty_sum
            + jnp.einsum(
                "trc,tco->ro",
                shifted_stack(shard_piece, True),
                weight,
                preferred_element_type=jnp.float32,
            ),
            lambda: empty_sum,
        )
        output = (values + conv_out.reshape(act_shape)).astype(jnp.bfloat16)
        saved_inputs = put_slot(saved_inputs, inputs, slot_index, active)
        saved_mean = put_slot(saved_mean, group_mean, slot_index, active)
        saved_rstd = put_slot(saved_rstd, group_rstd, slot_index, active)
        outgoing = put_slot(stack_recv, output, level, True)
        next_stack = shifted(outgoing, "segment", 1)
        return (next_stack, saved_inputs, saved_mean, saved_rstd, saved_full)

    zero_stack = jnp.zeros((half_way,) + act_shape, jnp.bfloat16)
    zero_buffer = jnp.zeros((micro_count,) + act_shape, jnp.bfloat16)
    zero_stats = jnp.zeros((micro_count, images, local_groups), jnp.float32)
    full_init = jnp.zeros((1,), jnp.bfloat16)
    forward_state = lax.fori_loop(
        0, tick_count, forward_tick, (zero_stack, zero_buffer, zero_stats, zero_stats, full_init)
    )
    saved_inputs, saved_mean, saved_rstd, saved_full = (
        forward_state[1],
        forward_state[2],
        forward_state[3],
        forward_state[4],
    )

    def backward_tick(tick_index, loop_state):
        grad_stack, grad_weight, grad_gain, grad_bias = loop_state
        micro_index = tick_index - bwd_place
        active = (micro_index >= 0) & (micro_index < micro_count)
        slot_index = jnp.clip(micro_index, 0, micro_count - 1)
        own_part = take_slot(grad_stack, level).astype(jnp.float32)
        later_part = jnp.where(
            has_above, take_slot(grad_stack, above_slot).astype(jnp.float32), 0.0
        )
        down_grad = (own_part + later_part).astype(jnp.bfloat16)
        up_grad = jnp.where(
            level == 0, take_slot(d_output, slot_index), take_slot(grad_stack, before_slot)
        )
        grad_out = jnp.where(is_down, down_grad, up_grad)
        values = take_slot(saved_inputs, slot_index).astype(jnp.float32)
        group_mean = take_slot(saved_mean, slot_index)
        group_rstd = take_slot(saved_rstd, slot_index)
        normed, pre_act = normalize(values, group_mean, group_rstd)
        sigma = jax.nn.sigmoid(pre_act)
        grad_rows = grad_out.reshape(row_count, local_width)
        hidden = (pre_act * sigma).astype(jnp.bfloat16)
        shard_piece = lax.all_gather(hidden, "chan", axis=2, tiled=True)
        grad_weight = grad_weight + lax.cond(
            active,
            lambda: jnp.einsum(
                "trc,ro->tco",
                shifted_stack(shard_piece, True),
                grad_rows,
                preferred_element_type=jnp.float32,
            ),
            lambda: jnp.zeros((9, shard_piece.shape[2], local_width), jnp.float32),
        )
        partial_grad = lax.cond(
            active,
            lambda: jnp.einsum(
                "tro,tco->rc",
                shifted_stack(grad_out, False),
                weight,
                preferred_element_type=jnp.float32,
            ),
            lambda: jnp.zeros((row_count, full_width), jnp.float32),
        )
        grad_hidden = lax.psum_scatter(
            partial_grad.reshape(images, pixels, full_width).astype(jnp.bfloat16),
            "chan",
            scatter_dimension=2,
            tiled=True,
        ).astype(jnp.float32)
        grad_pre = grad_hidden * sigma * (1.0 + pre_act * (1.0 - sigma))
        grad_gain = grad_gain + jnp.where(active, jnp.sum(grad_pre * normed, axis=(0, 1)), 0.0)
        grad_bias = grad_bias + jnp.where(active, jnp.sum(grad_pre, axis=(0, 1)), 0.0)
        grad_normed = grad_pre * gain_row
        first_mean = expand_groups(group_sums(grad_normed, group_width) / group_count, group_width)
        second_mean = expand_groups(
            group_sums(grad_normed * normed, group_width) / group_count, group_width
        )
        grad_in = (
            grad_out.astype(jnp.float32)
            + expand_groups(group_rstd, group_width)
            * (grad_normed - first_mean - normed * second_mean)
        ).astype(jnp.bfloat16)
        outgoing = put_slot(grad_stack, grad_in, level, True)
        next_stack = shifted(outgoing, "segment", -1)
        return (next_stack, grad_weight, grad_gain, grad_bias)

    backward_init = (
        zero_stack,
        jnp.zeros(weight.shape, jnp.float32),
        jnp.zeros((local_width,), jnp.float32),
        jnp.zeros((local_width,), jnp.float32),
    )
    backward_state = lax.fori_loop(0, tick_count, backward_tick, backward_init)
    grad_weight, grad_gain, grad_bias = (
        lax.psum(backward_state[1].astype(jnp.bfloat16), "dp").astype(jnp.float32),
        lax.psum(backward_state[2].astype(jnp.bfloat16), "dp").astype(jnp.float32),
        lax.psum(backward_state[3].astype(jnp.bfloat16), "dp").astype(jnp.float32),
    )
    return (grad_weight[None], grad_gain[None], grad_bias[None])


def solution(mesh):
    in_specs = (
        P(None, "dp", None, "chan"),
        P(None, "dp", None, "chan"),
        P("segment", None, None, "chan"),
        P("segment", "chan"),
        P("segment", "chan"),
    )
    out_specs = (P("segment", None, None, "chan"), P("segment", "chan"), P("segment", "chan"))
    return jax.shard_map(local, mesh=mesh, in_specs=in_specs, out_specs=out_specs, check_vma=False)
```

profile of v0, /device:TPU:1, one launch (start us, length us, event | category | flops | bytes accessed | tf_op | source)
XLA Modules:
  0.0 1573.2 jit_solution(6133271358537587081)
XLA Ops:
  8.2 388.7 %while.47 = (s32[]{:T(128)}, bf16[4,1,256,128]{3,2,1,0:T(8,128)(2,1)S(1)}, bf16[4,1,256,128]{3,2,1,0:T(8,128)(2,1)S(1)}, f32[4,1,4]{2,1,0:T(1,128)S(1)}, f32[4,1...) while((s32[]{:T(128)}, ...), condition=%wide.region_7.8_spmd, body=%wide.region_0.7_spmd.sunk | while | flops 604864512 | bytes 33960956 | solution.py:127
  10.7 16.7 %all_gather.25 = bf16[1,256,1024]{2,1,0:T(8,128)(2,1)S(1)} all-gather(bf16[1,256,128]{2,1,0:T(8,128)(2,1)S(1)} %fusion.67), channel_id=1, replica_groups=mesh['dp'=4,'segment'=8,'chan'=8] {'chan'}, dimensions={2}, use_global_device_ids=true | all-gather | bytes 589824 | tf_op jit(solution)/shard_map/while/body/eval_jaxpr/all_gather | solution.py:103
  40.8 14.4 all_gather.25
  71.2 14.9 all_gather.25
  102.1 14.9 all_gather.25
  132.9 14.9 all_gather.25
  147.8 13.5 collective-permute-start
  169.4 14.9 all_gather.25
  184.3 14.2 collective-permute-start
  206.6 14.9 all_gather.25
  221.5 14.1 collective-permute-start
  243.7 14.9 all_gather.25
  258.6 14.1 collective-permute-start
  280.7 14.9 all_gather.25
  295.7 17.8 %collective-permute-start = (bf16[4,1,256,128]{3,2,1,0:T(8,128)(2,1)S(1)}, bf16[4,1,256,128]{3,2,1,0:T(8,128)(2,1)S(1)}, u32[]{:S(2)}, u32[]{:S(2)}) collective-permute-start(bf16[4,1,256,128]{3,2,1,0:T(8,128)(2,1)S(1)} %fusion.68), channel_id=1, source_target_pairs={{0,8},{8,16},{16,24},{24,32},{32,40},{40,48},{48,56},{1,9},{9,17},... | collective-permute-start | bytes 786440 | tf_op jit(solution)/shard_map/while/body/eval_jaxpr/ppermute | solution.py:14
  321.5 14.9 all_gather.25
  336.5 14.1 collective-permute-start
  358.6 14.9 all_gather.25
  373.6 17.8 %collective-permute-start = (bf16[4,1,256,128]{3,2,1,0:T(8,128)(2,1)S(1)}, bf16[4,1,256,128]{3,2,1,0:T(8,128)(2,1)S(1)}, u32[]{:S(2)}, u32[]{:S(2)}) collective-permute-start(bf16[4,1,256,128]{3,2,1,0:T(8,128)(2,1)S(1)} %fusion.68), channel_id=1, source_target_pairs={{0,8},{8,16},{16,24},{24,32},{32,40},{40,48},{48,56},{1,9},{9,17},... | collective-permute-start | bytes 786440 | tf_op jit(solution)/shard_map/while/body/eval_jaxpr/ppermute | solution.py:14
  397.6 1098.8 %while.48 = (s32[]{:T(128)}, bf16[4,1,256,128]{3,2,1,0:T(8,128)(2,1)}, f32[9,1024,128]{2,1,0:T(8,128)}, f32[128]{0:T(128)S(1)}, f32[128]{0:T(128)S(1)}, /*index=...) while((s32[]{:T(128)}, ...), condition=%wide.region_20.21_spmd.clone, body=%wide.region_8.20_spmd.clone.sunk | while | flops 1211728384 | bytes 62218040 | solution.py:208
  400.9 69.3 %reduce-scatter.6.cloned.1.call-done = bf16[128,256]{1,0:T(8,128)(2,1)} async-done(((bf16[1024,256]{1,0:T(8,128)(2,1)}), bf16[128,256]{1,0:T(8,128)(2,1)}) %reduce-scatter.6.cloned.1.call-update) | async-done | bytes 65552 | tf_op jit(solution)/shard_map/while
  474.1 19.5 %all_gather.26 = bf16[1,256,1024]{2,1,0:T(8,128)(2,1)S(1)} all-gather(bf16[1,256,128]{2,1,0:T(8,128)(2,1)S(1)} %get-tuple-element.1489), channel_id=1, replica_groups=mesh['dp'=4,'segment'=8,'chan'=8] {'chan'}, dimensions={2}, use_global_device_ids=true | all-gather | bytes 589824 | tf_op jit(solution)/shard_map/while/body/eval_jaxpr/all_gather | solution.py:158
  506.2 58.9 %reduce-scatter.6.cloned.1.call-done = bf16[128,256]{1,0:T(8,128)(2,1)} async-done(((bf16[1024,256]{1,0:T(8,128)(2,1)}), bf16[128,256]{1,0:T(8,128)(2,1)}) %reduce-scatter.6.cloned.1.call-update) | async-done | bytes 65552 | tf_op jit(solution)/shard_map/while
  569.0 19.5 %all_gather.26 = bf16[1,256,1024]{2,1,0:T(8,128)(2,1)S(1)} all-gather(bf16[1,256,128]{2,1,0:T(8,128)(2,1)S(1)} %get-tuple-element.1489), channel_id=1, replica_groups=mesh['dp'=4,'segment'=8,'chan'=8] {'chan'}, dimensions={2}, use_global_device_ids=true | all-gather | bytes 589824 | tf_op jit(solution)/shard_map/while/body/eval_jaxpr/all_gather | solution.py:158
  602.5 58.7 %reduce-scatter.6.cloned.1.call-done = bf16[128,256]{1,0:T(8,128)(2,1)} async-done(((bf16[1024,256]{1,0:T(8,128)(2,1)}), bf16[128,256]{1,0:T(8,128)(2,1)}) %reduce-scatter.6.cloned.1.call-update) | async-done | bytes 65552 | tf_op jit(solution)/shard_map/while
  665.1 19.6 %all_gather.26 = bf16[1,256,1024]{2,1,0:T(8,128)(2,1)S(1)} all-gather(bf16[1,256,128]{2,1,0:T(8,128)(2,1)S(1)} %get-tuple-element.1489), channel_id=1, replica_groups=mesh['dp'=4,'segment'=8,'chan'=8] {'chan'}, dimensions={2}, use_global_device_ids=true | all-gather | bytes 589824 | tf_op jit(solution)/shard_map/while/body/eval_jaxpr/all_gather | solution.py:158
  698.7 58.8 %reduce-scatter.6.cloned.1.call-done = bf16[128,256]{1,0:T(8,128)(2,1)} async-done(((bf16[1024,256]{1,0:T(8,128)(2,1)}), bf16[128,256]{1,0:T(8,128)(2,1)}) %reduce-scatter.6.cloned.1.call-update) | async-done | bytes 65552 | tf_op jit(solution)/shard_map/while
  761.4 19.6 %all_gather.26 = bf16[1,256,1024]{2,1,0:T(8,128)(2,1)S(1)} all-gather(bf16[1,256,128]{2,1,0:T(8,128)(2,1)S(1)} %get-tuple-element.1489), channel_id=1, replica_groups=mesh['dp'=4,'segment'=8,'chan'=8] {'chan'}, dimensions={2}, use_global_device_ids=true | all-gather | bytes 589824 | tf_op jit(solution)/shard_map/while/body/eval_jaxpr/all_gather | solution.py:158
  795.1 63.4 %reduce-scatter.6.cloned.1.call-done = bf16[128,256]{1,0:T(8,128)(2,1)} async-done(((bf16[1024,256]{1,0:T(8,128)(2,1)}), bf16[128,256]{1,0:T(8,128)(2,1)}) %reduce-scatter.6.cloned.1.call-update) | async-done | bytes 65552 | tf_op jit(solution)/shard_map/while
  862.4 19.8 %all_gather.26 = bf16[1,256,1024]{2,1,0:T(8,128)(2,1)S(1)} all-gather(bf16[1,256,128]{2,1,0:T(8,128)(2,1)S(1)} %get-tuple-element.1489), channel_id=1, replica_groups=mesh['dp'=4,'segment'=8,'chan'=8] {'chan'}, dimensions={2}, use_global_device_ids=true | all-gather | bytes 589824 | tf_op jit(solution)/shard_map/while/body/eval_jaxpr/all_gather | solution.py:158
  896.1 63.4 %reduce-scatter.6.cloned.1.call-done = bf16[128,256]{1,0:T(8,128)(2,1)} async-done(((bf16[1024,256]{1,0:T(8,128)(2,1)}), bf16[128,256]{1,0:T(8,128)(2,1)}) %reduce-scatter.6.cloned.1.call-update) | async-done | bytes 65552 | tf_op jit(solution)/shard_map/while
  963.5 19.5 %all_gather.26 = bf16[1,256,1024]{2,1,0:T(8,128)(2,1)S(1)} all-gather(bf16[1,256,128]{2,1,0:T(8,128)(2,1)S(1)} %get-tuple-element.1489), channel_id=1, replica_groups=mesh['dp'=4,'segment'=8,'chan'=8] {'chan'}, dimensions={2}, use_global_device_ids=true | all-gather | bytes 589824 | tf_op jit(solution)/shard_map/while/body/eval_jaxpr/all_gather | solution.py:158
  997.0 63.4 %reduce-scatter.6.cloned.1.call-done = bf16[128,256]{1,0:T(8,128)(2,1)} async-done(((bf16[1024,256]{1,0:T(8,128)(2,1)}), bf16[128,256]{1,0:T(8,128)(2,1)}) %reduce-scatter.6.cloned.1.call-update) | async-done | bytes 65552 | tf_op jit(solution)/shard_map/while
  1064.3 19.6 %all_gather.26 = bf16[1,256,1024]{2,1,0:T(8,128)(2,1)S(1)} all-gather(bf16[1,256,128]{2,1,0:T(8,128)(2,1)S(1)} %get-tuple-element.1489), channel_id=1, replica_groups=mesh['dp'=4,'segment'=8,'chan'=8] {'chan'}, dimensions={2}, use_global_device_ids=true | all-gather | bytes 589824 | tf_op jit(solution)/shard_map/while/body/eval_jaxpr/all_gather | solution.py:158
  1100.7 58.3 %reduce-scatter.6.cloned.1.call-done = bf16[128,256]{1,0:T(8,128)(2,1)} async-done(((bf16[1024,256]{1,0:T(8,128)(2,1)}), bf16[128,256]{1,0:T(8,128)(2,1)}) %reduce-scatter.6.cloned.1.call-update) | async-done | bytes 65552 | tf_op jit(solution)/shard_map/while
  1162.9 19.5 %all_gather.26 = bf16[1,256,1024]{2,1,0:T(8,128)(2,1)S(1)} all-gather(bf16[1,256,128]{2,1,0:T(8,128)(2,1)S(1)} %get-tuple-element.1489), channel_id=1, replica_groups=mesh['dp'=4,'segment'=8,'chan'=8] {'chan'}, dimensions={2}, use_global_device_ids=true | all-gather | bytes 589824 | tf_op jit(solution)/shard_map/while/body/eval_jaxpr/all_gather | solution.py:158
  1182.4 27.5 %conditional.10 = (f32[9,1024,128]{2,1,0:T(8,128)}) conditional(s32[]{:T(128)} %convert_element_type.631, () %tuple.163, (bf16[1,256,1024]{2,1,0:T(8,128)(2,1)S(1)}, pred[]{:T(512)}, pred[]{:T(512)}, bf16[1,1,256,128]{3,2,1,0:T(8,128)(2,1)S(1)}, bf16[1,1,256,128]{3,2,1,0:T(8,128)(2,1)S(1)}, ...), branch_computations={%region_16.16_spmd, %region_17.17_spmd} | conditional | flops 604045312 | bytes 33226762 | solution.py:159
  1224.1 28.5 %reduce-scatter.6.cloned.1.call-done = bf16[128,256]{1,0:T(8,128)(2,1)} async-done(((bf16[1024,256]{1,0:T(8,128)(2,1)}), bf16[128,256]{1,0:T(8,128)(2,1)}) %reduce-scatter.6.cloned.1.call-update) | async-done | bytes 65552 | tf_op jit(solution)/shard_map/while
  1256.4 19.6 %all_gather.26 = bf16[1,256,1024]{2,1,0:T(8,128)(2,1)S(1)} all-gather(bf16[1,256,128]{2,1,0:T(8,128)(2,1)S(1)} %get-tuple-element.1489), channel_id=1, replica_groups=mesh['dp'=4,'segment'=8,'chan'=8] {'chan'}, dimensions={2}, use_global_device_ids=true | all-gather | bytes 589824 | tf_op jit(solution)/shard_map/while/body/eval_jaxpr/all_gather | solution.py:158
  1276.1 27.5 %conditional.10 = (f32[9,1024,128]{2,1,0:T(8,128)}) conditional(s32[]{:T(128)} %convert_element_type.631, () %tuple.163, (bf16[1,256,1024]{2,1,0:T(8,128)(2,1)S(1)}, pred[]{:T(512)}, pred[]{:T(512)}, bf16[1,1,256,128]{3,2,1,0:T(8,128)(2,1)S(1)}, bf16[1,1,256,128]{3,2,1,0:T(8,128)(2,1)S(1)}, ...), branch_computations={%region_16.16_spmd, %region_17.17_spmd} | conditional | flops 604045312 | bytes 33226762 | solution.py:159
  1317.8 27.1 %reduce-scatter.6.cloned.1.call-done = bf16[128,256]{1,0:T(8,128)(2,1)} async-done(((bf16[1024,256]{1,0:T(8,128)(2,1)}), bf16[128,256]{1,0:T(8,128)(2,1)}) %reduce-scatter.6.cloned.1.call-update) | async-done | bytes 65552 | tf_op jit(solution)/shard_map/while
  1348.7 19.6 %all_gather.26 = bf16[1,256,1024]{2,1,0:T(8,128)(2,1)S(1)} all-gather(bf16[1,256,128]{2,1,0:T(8,128)(2,1)S(1)} %get-tuple-element.1489), channel_id=1, replica_groups=mesh['dp'=4,'segment'=8,'chan'=8] {'chan'}, dimensions={2}, use_global_device_ids=true | all-gather | bytes 589824 | tf_op jit(solution)/shard_map/while/body/eval_jaxpr/all_gather | solution.py:158
  1368.4 27.5 %conditional.10 = (f32[9,1024,128]{2,1,0:T(8,128)}) conditional(s32[]{:T(128)} %convert_element_type.631, () %tuple.163, (bf16[1,256,1024]{2,1,0:T(8,128)(2,1)S(1)}, pred[]{:T(512)}, pred[]{:T(512)}, bf16[1,1,256,128]{3,2,1,0:T(8,128)(2,1)S(1)}, bf16[1,1,256,128]{3,2,1,0:T(8,128)(2,1)S(1)}, ...), branch_computations={%region_16.16_spmd, %region_17.17_spmd} | conditional | flops 604045312 | bytes 33226762 | solution.py:159
  1410.1 27.1 %reduce-scatter.6.cloned.1.call-done = bf16[128,256]{1,0:T(8,128)(2,1)} async-done(((bf16[1024,256]{1,0:T(8,128)(2,1)}), bf16[128,256]{1,0:T(8,128)(2,1)}) %reduce-scatter.6.cloned.1.call-update) | async-done | bytes 65552 | tf_op jit(solution)/shard_map/while
  1441.0 19.8 %all_gather.26 = bf16[1,256,1024]{2,1,0:T(8,128)(2,1)S(1)} all-gather(bf16[1,256,128]{2,1,0:T(8,128)(2,1)S(1)} %get-tuple-element.1489), channel_id=1, replica_groups=mesh['dp'=4,'segment'=8,'chan'=8] {'chan'}, dimensions={2}, use_global_device_ids=true | all-gather | bytes 589824 | tf_op jit(solution)/shard_map/while/body/eval_jaxpr/all_gather | solution.py:158
  1460.8 27.5 %conditional.10 = (f32[9,1024,128]{2,1,0:T(8,128)}) conditional(s32[]{:T(128)} %convert_element_type.631, () %tuple.163, (bf16[1,256,1024]{2,1,0:T(8,128)(2,1)S(1)}, pred[]{:T(512)}, pred[]{:T(512)}, bf16[1,1,256,128]{3,2,1,0:T(8,128)(2,1)S(1)}, bf16[1,1,256,128]{3,2,1,0:T(8,128)(2,1)S(1)}, ...), branch_computations={%region_16.16_spmd, %region_17.17_spmd} | conditional | flops 604045312 | bytes 33226762 | solution.py:159
  1500.6 8.8 all-reduce.3
  1510.4 51.4 %all-reduce.6.cloned.1.call-done = bf16[1,9,1024,128]{3,2,1,0:T(8,128)(2,1)} async-done(((bf16[1,9,1024,128]{3,2,1,0:T(8,128)(2,1)}), bf16[1,9,1024,128]{3,2,1,0:T(8,128)(2,1)}) %all-reduce.6.cloned.1.call-update) | async-done | bytes 2359312 | tf_op jit(solution)/shard_map/psum | solution.py:210
  (861 shorter events, 476.6 us)
Async XLA Ops:
  31.2 7.1 collective-permute-start
  59.0 9.6 collective-permute-start
  89.9 9.6 collective-permute-start
  120.7 9.6 collective-permute-start
  147.8 19.0 %collective-permute-start = (bf16[4,1,256,128]{3,2,1,0:T(8,128)(2,1)S(1)}, bf16[4,1,256,128]{3,2,1,0:T(8,128)(2,1)S(1)}, u32[]{:S(2)}, u32[]{:S(2)}) collective-permute-start(bf16[4,1,256,128]{3,2,1,0:T(8,128)(2,1)S(1)} %fusion.68), channel_id=1, source_target_pairs={{0,8},{8,16},{16,24},{24,32},{32,40},{40,48},{48,56},{1,9},{9,17},... | collective-permute-start | bytes 786440 | tf_op jit(solution)/shard_map/while/body/eval_jaxpr/ppermute | solution.py:14
  184.3 19.7 %collective-permute-start = (bf16[4,1,256,128]{3,2,1,0:T(8,128)(2,1)S(1)}, bf16[4,1,256,128]{3,2,1,0:T(8,128)(2,1)S(1)}, u32[]{:S(2)}, u32[]{:S(2)}) collective-permute-start(bf16[4,1,256,128]{3,2,1,0:T(8,128)(2,1)S(1)} %fusion.68), channel_id=1, source_target_pairs={{0,8},{8,16},{16,24},{24,32},{32,40},{40,48},{48,56},{1,9},{9,17},... | collective-permute-start | bytes 786440 | tf_op jit(solution)/shard_map/while/body/eval_jaxpr/ppermute | solution.py:14
  221.5 19.6 %collective-permute-start = (bf16[4,1,256,128]{3,2,1,0:T(8,128)(2,1)S(1)}, bf16[4,1,256,128]{3,2,1,0:T(8,128)(2,1)S(1)}, u32[]{:S(2)}, u32[]{:S(2)}) collective-permute-start(bf16[4,1,256,128]{3,2,1,0:T(8,128)(2,1)S(1)} %fusion.68), channel_id=1, source_target_pairs={{0,8},{8,16},{16,24},{24,32},{32,40},{40,48},{48,56},{1,9},{9,17},... | collective-permute-start | bytes 786440 | tf_op jit(solution)/shard_map/while/body/eval_jaxpr/ppermute | solution.py:14
  258.6 19.6 %collective-permute-start = (bf16[4,1,256,128]{3,2,1,0:T(8,128)(2,1)S(1)}, bf16[4,1,256,128]{3,2,1,0:T(8,128)(2,1)S(1)}, u32[]{:S(2)}, u32[]{:S(2)}) collective-permute-start(bf16[4,1,256,128]{3,2,1,0:T(8,128)(2,1)S(1)} %fusion.68), channel_id=1, source_target_pairs={{0,8},{8,16},{16,24},{24,32},{32,40},{40,48},{48,56},{1,9},{9,17},... | collective-permute-start | bytes 786440 | tf_op jit(solution)/shard_map/while/body/eval_jaxpr/ppermute | solution.py:14
  295.7 23.3 %collective-permute-start = (bf16[4,1,256,128]{3,2,1,0:T(8,128)(2,1)S(1)}, bf16[4,1,256,128]{3,2,1,0:T(8,128)(2,1)S(1)}, u32[]{:S(2)}, u32[]{:S(2)}) collective-permute-start(bf16[4,1,256,128]{3,2,1,0:T(8,128)(2,1)S(1)} %fusion.68), channel_id=1, source_target_pairs={{0,8},{8,16},{16,24},{24,32},{32,40},{40,48},{48,56},{1,9},{9,17},... | collective-permute-start | bytes 786440 | tf_op jit(solution)/shard_map/while/body/eval_jaxpr/ppermute | solution.py:14
  336.5 19.6 %collective-permute-start = (bf16[4,1,256,128]{3,2,1,0:T(8,128)(2,1)S(1)}, bf16[4,1,256,128]{3,2,1,0:T(8,128)(2,1)S(1)}, u32[]{:S(2)}, u32[]{:S(2)}) collective-permute-start(bf16[4,1,256,128]{3,2,1,0:T(8,128)(2,1)S(1)} %fusion.68), channel_id=1, source_target_pairs={{0,8},{8,16},{16,24},{24,32},{32,40},{40,48},{48,56},{1,9},{9,17},... | collective-permute-start | bytes 786440 | tf_op jit(solution)/shard_map/while/body/eval_jaxpr/ppermute | solution.py:14
  373.6 23.3 %collective-permute-start = (bf16[4,1,256,128]{3,2,1,0:T(8,128)(2,1)S(1)}, bf16[4,1,256,128]{3,2,1,0:T(8,128)(2,1)S(1)}, u32[]{:S(2)}, u32[]{:S(2)}) collective-permute-start(bf16[4,1,256,128]{3,2,1,0:T(8,128)(2,1)S(1)} %fusion.68), channel_id=1, source_target_pairs={{0,8},{8,16},{16,24},{24,32},{32,40},{40,48},{48,56},{1,9},{9,17},... | collective-permute-start | bytes 786440 | tf_op jit(solution)/shard_map/while/body/eval_jaxpr/ppermute | solution.py:14
  397.6 74.5 %copy-start.1 = (bf16[4,1,256,128]{3,2,1,0:T(8,128)(2,1)}, bf16[4,1,256,128]{3,2,1,0:T(8,128)(2,1)S(1)}, u32[]{:S(2)}) copy-start(bf16[4,1,256,128]{3,2,1,0:T(8,128)(2,1)S(1)} %get-tuple-element.1623) | copy-start | bytes 786436 | tf_op jit(solution)/shard_map/while
  397.6 72.6 %reduce-scatter.6.cloned.1.call-start = ((), (), s32[]{:S(2)}) async-start(), calls=%async_computation.2 | async-start | bytes 589824 | tf_op jit(solution)/shard_map/while
  398.7 72.5 %copy-start.3 = (f32[1,128]{1,0:T(1,128)S(1)}, f32[1,128]{1,0:T(1,128)}, u32[]{:S(2)}) copy-start(f32[1,128]{1,0:T(1,128)} %get-tuple-element.1625) | copy-start | bytes 1540 | tf_op jit(solution)/shard_map/while
  398.7 72.5 %copy-start.4 = (f32[1,128]{1,0:T(1,128)S(1)}, f32[1,128]{1,0:T(1,128)}, u32[]{:S(2)}) copy-start(f32[1,128]{1,0:T(1,128)} %get-tuple-element.1626) | copy-start | bytes 1540 | tf_op jit(solution)/shard_map/while
  472.8 28.4 %collective-permute-start.1 = (bf16[4,1,256,128]{3,2,1,0:T(8,128)(2,1)}, bf16[4,1,256,128]{3,2,1,0:T(8,128)(2,1)}, u32[]{:S(2)}, u32[]{:S(2)}) collective-permute-start(bf16[4,1,256,128]{3,2,1,0:T(8,128)(2,1)} %fusion.72), channel_id=1, source_target_pairs={{8,0},{16,8},{24,16},{32,24},{40,32},{48,40},{56,48},{9,1},{17,9},... | collective-permute-start | bytes 786440 | tf_op jit(solution)/shard_map/while/body/eval_jaxpr/ppermute | solution.py:14
  502.9 62.2 %reduce-scatter.6.cloned.1.call-start = ((), (), s32[]{:S(2)}) async-start(), calls=%async_computation.2 | async-start | bytes 589824 | tf_op jit(solution)/shard_map/while
  567.7 29.8 %collective-permute-start.1 = (bf16[4,1,256,128]{3,2,1,0:T(8,128)(2,1)}, bf16[4,1,256,128]{3,2,1,0:T(8,128)(2,1)}, u32[]{:S(2)}, u32[]{:S(2)}) collective-permute-start(bf16[4,1,256,128]{3,2,1,0:T(8,128)(2,1)} %fusion.72), channel_id=1, source_target_pairs={{8,0},{16,8},{24,16},{32,24},{40,32},{48,40},{56,48},{9,1},{17,9},... | collective-permute-start | bytes 786440 | tf_op jit(solution)/shard_map/while/body/eval_jaxpr/ppermute | solution.py:14
  599.2 62.0 %reduce-scatter.6.cloned.1.call-start = ((), (), s32[]{:S(2)}) async-start(), calls=%async_computation.2 | async-start | bytes 589824 | tf_op jit(solution)/shard_map/while
  663.8 29.9 %collective-permute-start.1 = (bf16[4,1,256,128]{3,2,1,0:T(8,128)(2,1)}, bf16[4,1,256,128]{3,2,1,0:T(8,128)(2,1)}, u32[]{:S(2)}, u32[]{:S(2)}) collective-permute-start(bf16[4,1,256,128]{3,2,1,0:T(8,128)(2,1)} %fusion.72), channel_id=1, source_target_pairs={{8,0},{16,8},{24,16},{32,24},{40,32},{48,40},{56,48},{9,1},{17,9},... | collective-permute-start | bytes 786440 | tf_op jit(solution)/shard_map/while/body/eval_jaxpr/ppermute | solution.py:14
  695.4 62.1 %reduce-scatter.6.cloned.1.call-start = ((), (), s32[]{:S(2)}) async-start(), calls=%async_computation.2 | async-start | bytes 589824 | tf_op jit(solution)/shard_map/while
  760.1 29.9 %collective-permute-start.1 = (bf16[4,1,256,128]{3,2,1,0:T(8,128)(2,1)}, bf16[4,1,256,128]{3,2,1,0:T(8,128)(2,1)}, u32[]{:S(2)}, u32[]{:S(2)}) collective-permute-start(bf16[4,1,256,128]{3,2,1,0:T(8,128)(2,1)} %fusion.72), channel_id=1, source_target_pairs={{8,0},{16,8},{24,16},{32,24},{40,32},{48,40},{56,48},{9,1},{17,9},... | collective-permute-start | bytes 786440 | tf_op jit(solution)/shard_map/while/body/eval_jaxpr/ppermute | solution.py:14
  791.8 68.6 %copy-start.1 = (bf16[4,1,256,128]{3,2,1,0:T(8,128)(2,1)}, bf16[4,1,256,128]{3,2,1,0:T(8,128)(2,1)S(1)}, u32[]{:S(2)}) copy-start(bf16[4,1,256,128]{3,2,1,0:T(8,128)(2,1)S(1)} %get-tuple-element.1623) | copy-start | bytes 786436 | tf_op jit(solution)/shard_map/while
  791.8 66.7 %reduce-scatter.6.cloned.1.call-start = ((), (), s32[]{:S(2)}) async-start(), calls=%async_computation.2 | async-start | bytes 589824 | tf_op jit(solution)/shard_map/while
  792.8 66.7 %copy-start.3 = (f32[1,128]{1,0:T(1,128)S(1)}, f32[1,128]{1,0:T(1,128)}, u32[]{:S(2)}) copy-start(f32[1,128]{1,0:T(1,128)} %get-tuple-element.1625) | copy-start | bytes 1540 | tf_op jit(solution)/shard_map/while
  792.9 66.7 %copy-start.4 = (f32[1,128]{1,0:T(1,128)S(1)}, f32[1,128]{1,0:T(1,128)}, u32[]{:S(2)}) copy-start(f32[1,128]{1,0:T(1,128)} %get-tuple-element.1626) | copy-start | bytes 1540 | tf_op jit(solution)/shard_map/while
  861.1 30.1 %collective-permute-start.1 = (bf16[4,1,256,128]{3,2,1,0:T(8,128)(2,1)}, bf16[4,1,256,128]{3,2,1,0:T(8,128)(2,1)}, u32[]{:S(2)}, u32[]{:S(2)}) collective-permute-start(bf16[4,1,256,128]{3,2,1,0:T(8,128)(2,1)} %fusion.72), channel_id=1, source_target_pairs={{8,0},{16,8},{24,16},{32,24},{40,32},{48,40},{56,48},{9,1},{17,9},... | collective-permute-start | bytes 786440 | tf_op jit(solution)/shard_map/while/body/eval_jaxpr/ppermute | solution.py:14
  892.8 68.7 %copy-start.1 = (bf16[4,1,256,128]{3,2,1,0:T(8,128)(2,1)}, bf16[4,1,256,128]{3,2,1,0:T(8,128)(2,1)S(1)}, u32[]{:S(2)}) copy-start(bf16[4,1,256,128]{3,2,1,0:T(8,128)(2,1)S(1)} %get-tuple-element.1623) | copy-start | bytes 786436 | tf_op jit(solution)/shard_map/while
  892.8 66.7 %reduce-scatter.6.cloned.1.call-start = ((), (), s32[]{:S(2)}) async-start(), calls=%async_computation.2 | async-start | bytes 589824 | tf_op jit(solution)/shard_map/while
  893.9 66.7 %copy-start.3 = (f32[1,128]{1,0:T(1,128)S(1)}, f32[1,128]{1,0:T(1,128)}, u32[]{:S(2)}) copy-start(f32[1,128]{1,0:T(1,128)} %get-tuple-element.1625) | copy-start | bytes 1540 | tf_op jit(solution)/shard_map/while
  893.9 66.7 %copy-start.4 = (f32[1,128]{1,0:T(1,128)S(1)}, f32[1,128]{1,0:T(1,128)}, u32[]{:S(2)}) copy-start(f32[1,128]{1,0:T(1,128)} %get-tuple-element.1626) | copy-start | bytes 1540 | tf_op jit(solution)/shard_map/while
  962.2 29.8 %collective-permute-start.1 = (bf16[4,1,256,128]{3,2,1,0:T(8,128)(2,1)}, bf16[4,1,256,128]{3,2,1,0:T(8,128)(2,1)}, u32[]{:S(2)}, u32[]{:S(2)}) collective-permute-start(bf16[4,1,256,128]{3,2,1,0:T(8,128)(2,1)} %fusion.72), channel_id=1, source_target_pairs={{8,0},{16,8},{24,16},{32,24},{40,32},{48,40},{56,48},{9,1},{17,9},... | collective-permute-start | bytes 786440 | tf_op jit(solution)/shard_map/while/body/eval_jaxpr/ppermute | solution.py:14
  993.7 68.6 %copy-start.1 = (bf16[4,1,256,128]{3,2,1,0:T(8,128)(2,1)}, bf16[4,1,256,128]{3,2,1,0:T(8,128)(2,1)S(1)}, u32[]{:S(2)}) copy-start(bf16[4,1,256,128]{3,2,1,0:T(8,128)(2,1)S(1)} %get-tuple-element.1623) | copy-start | bytes 786436 | tf_op jit(solution)/shard_map/while
  993.7 66.7 %reduce-scatter.6.cloned.1.call-start = ((), (), s32[]{:S(2)}) async-start(), calls=%async_computation.2 | async-start | bytes 589824 | tf_op jit(solution)/shard_map/while
  994.8 66.6 %copy-start.3 = (f32[1,128]{1,0:T(1,128)S(1)}, f32[1,128]{1,0:T(1,128)}, u32[]{:S(2)}) copy-start(f32[1,128]{1,0:T(1,128)} %get-tuple-element.1625) | copy-start | bytes 1540 | tf_op jit(solution)/shard_map/while
  994.8 66.6 %copy-start.4 = (f32[1,128]{1,0:T(1,128)S(1)}, f32[1,128]{1,0:T(1,128)}, u32[]{:S(2)}) copy-start(f32[1,128]{1,0:T(1,128)} %get-tuple-element.1626) | copy-start | bytes 1540 | tf_op jit(solution)/shard_map/while
  1063.0 29.9 %collective-permute-start.1 = (bf16[4,1,256,128]{3,2,1,0:T(8,128)(2,1)}, bf16[4,1,256,128]{3,2,1,0:T(8,128)(2,1)}, u32[]{:S(2)}, u32[]{:S(2)}) collective-permute-start(bf16[4,1,256,128]{3,2,1,0:T(8,128)(2,1)} %fusion.72), channel_id=1, source_target_pairs={{8,0},{16,8},{24,16},{32,24},{40,32},{48,40},{56,48},{9,1},{17,9},... | collective-permute-start | bytes 786440 | tf_op jit(solution)/shard_map/while/body/eval_jaxpr/ppermute | solution.py:14
  1094.6 66.3 %copy-start.1 = (bf16[4,1,256,128]{3,2,1,0:T(8,128)(2,1)}, bf16[4,1,256,128]{3,2,1,0:T(8,128)(2,1)S(1)}, u32[]{:S(2)}) copy-start(bf16[4,1,256,128]{3,2,1,0:T(8,128)(2,1)S(1)} %get-tuple-element.1623) | copy-start | bytes 786436 | tf_op jit(solution)/shard_map/while
  1094.6 64.3 %reduce-scatter.6.cloned.1.call-start = ((), (), s32[]{:S(2)}) async-start(), calls=%async_computation.2 | async-start | bytes 589824 | tf_op jit(solution)/shard_map/while
  1095.7 64.3 %copy-start.3 = (f32[1,128]{1,0:T(1,128)S(1)}, f32[1,128]{1,0:T(1,128)}, u32[]{:S(2)}) copy-start(f32[1,128]{1,0:T(1,128)} %get-tuple-element.1625) | copy-start | bytes 1540 | tf_op jit(solution)/shard_map/while
  1161.6 54.7 %collective-permute-start.1 = (bf16[4,1,256,128]{3,2,1,0:T(8,128)(2,1)}, bf16[4,1,256,128]{3,2,1,0:T(8,128)(2,1)}, u32[]{:S(2)}, u32[]{:S(2)}) collective-permute-start(bf16[4,1,256,128]{3,2,1,0:T(8,128)(2,1)} %fusion.72), channel_id=1, source_target_pairs={{8,0},{16,8},{24,16},{32,24},{40,32},{48,40},{56,48},{9,1},{17,9},... | collective-permute-start | bytes 786440 | tf_op jit(solution)/shard_map/while/body/eval_jaxpr/ppermute | solution.py:14
  1218.0 34.5 %reduce-scatter.6.cloned.1.call-start = ((), (), s32[]{:S(2)}) async-start(), calls=%async_computation.2 | async-start | bytes 589824 | tf_op jit(solution)/shard_map/while
  1255.1 54.9 %collective-permute-start.1 = (bf16[4,1,256,128]{3,2,1,0:T(8,128)(2,1)}, bf16[4,1,256,128]{3,2,1,0:T(8,128)(2,1)}, u32[]{:S(2)}, u32[]{:S(2)}) collective-permute-start(bf16[4,1,256,128]{3,2,1,0:T(8,128)(2,1)} %fusion.72), channel_id=1, source_target_pairs={{8,0},{16,8},{24,16},{32,24},{40,32},{48,40},{56,48},{9,1},{17,9},... | collective-permute-start | bytes 786440 | tf_op jit(solution)/shard_map/while/body/eval_jaxpr/ppermute | solution.py:14
  1311.7 33.1 %reduce-scatter.6.cloned.1.call-start = ((), (), s32[]{:S(2)}) async-start(), calls=%async_computation.2 | async-start | bytes 589824 | tf_op jit(solution)/shard_map/while
  1347.5 54.9 %collective-permute-start.1 = (bf16[4,1,256,128]{3,2,1,0:T(8,128)(2,1)}, bf16[4,1,256,128]{3,2,1,0:T(8,128)(2,1)}, u32[]{:S(2)}, u32[]{:S(2)}) collective-permute-start(bf16[4,1,256,128]{3,2,1,0:T(8,128)(2,1)} %fusion.72), channel_id=1, source_target_pairs={{8,0},{16,8},{24,16},{32,24},{40,32},{48,40},{56,48},{9,1},{17,9},... | collective-permute-start | bytes 786440 | tf_op jit(solution)/shard_map/while/body/eval_jaxpr/ppermute | solution.py:14
  1404.0 33.1 %reduce-scatter.6.cloned.1.call-start = ((), (), s32[]{:S(2)}) async-start(), calls=%async_computation.2 | async-start | bytes 589824 | tf_op jit(solution)/shard_map/while
  1439.7 55.1 %collective-permute-start.1 = (bf16[4,1,256,128]{3,2,1,0:T(8,128)(2,1)}, bf16[4,1,256,128]{3,2,1,0:T(8,128)(2,1)}, u32[]{:S(2)}, u32[]{:S(2)}) collective-permute-start(bf16[4,1,256,128]{3,2,1,0:T(8,128)(2,1)} %fusion.72), channel_id=1, source_target_pairs={{8,0},{16,8},{24,16},{32,24},{40,32},{48,40},{56,48},{9,1},{17,9},... | collective-permute-start | bytes 786440 | tf_op jit(solution)/shard_map/while/body/eval_jaxpr/ppermute | solution.py:14
  1496.5 65.3 %all-reduce.6.cloned.1.call-start = ((), (), s32[]{:S(2)}) async-start(), calls=%async_computation.1 | async-start | bytes 4718592 | tf_op jit(solution)/shard_map/psum | solution.py:210
  (34 other events, 1031.6 us)
Sparse Core Ops, SparseCore 0:
  400.9 69.1 reduce-scatter.5
  506.2 58.8 reduce-scatter.5
  602.5 58.6 reduce-scatter.5
  698.5 58.9 reduce-scatter.5
  794.8 63.5 reduce-scatter.5
  895.9 63.5 reduce-scatter.5
  997.0 63.3 reduce-scatter.5
  1100.4 58.4 reduce-scatter.5
  1223.8 28.6 reduce-scatter.5
  1317.5 27.2 reduce-scatter.5
  1409.8 27.2 reduce-scatter.5
Sparse Core Ops, SparseCore 1:
  1500.7 61.0 all-reduce.5
where the time goes:
time: 1580 us; the launch traced here: 1570 us
  waiting for transfers between devices  688 us (44%)
  blocking collectives  389 us (25%)
  local copies, waits for them, and re-layouts  178 us (11%)
  starting transfers between devices  133 us (8%)
  other arithmetic  126 us (8%)
  matrix products  39.6 us (3%)
    while x22, waiting for transfers between devices  577 us
    all_gather x11, blocking collectives, backward_tick(): shard_piece = lax.all_gather(hidden, 'chan', axis=2, tiled=True)  216 us
    all_gather x11, blocking collectives, forward_tick(): shard_piece = lax.all_gather(hidden, 'chan', axis=2, tiled=True)  165 us
    ppermute x22, starting transfers between devices, shifted(): return lax.ppermute(shard, axis, pairs)  133 us
    add x11, other arithmetic, backward_tick(): grad_weight + lax.cond(active, lambda: jnp.einsum('trc,ro->tco', shifted_...  69.6 us
    ppermute x22, waiting for transfers between devices, shifted(): return lax.ppermute(shard, axis, pairs)  60.2 us
    psum x1, waiting for transfers between devices, local(): lax.psum(backward_state[1].astype(jnp.bfloat16), 'dp').astype(jnp.float32)  51.4 us
    cond x104, local copies, waits for them, and re-layouts  50.2 us
  transfers between devices with their start and end apart: 34, of which 23 were waited for; matrix products, arithmetic and copies ran while one was open for 13% of the time, Pallas kernels for 0%

commit v1 on v0

--- a/solution.py
+++ b/solution.py
@@ -155,7 +155,9 @@
         sigma = jax.nn.sigmoid(pre_act)
         grad_rows = grad_out.reshape(row_count, local_width)
         hidden = (pre_act * sigma).astype(jnp.bfloat16)
-        shard_piece = lax.all_gather(hidden, "chan", axis=2, tiled=True)
+        shard_piece = jnp.concatenate(
+            lax.all_to_all(jnp.stack([hidden] * lax.axis_size("chan")), "chan", 0, 0), axis=2
+        )
         grad_weight = grad_weight + lax.cond(
             active,
             lambda: jnp.einsum(

time: 1580 us -> 1320 us (0.84)
  blocking collectives: 389 us -> 172 us
  waiting for transfers between devices: 688 us -> 557 us
  starting transfers between devices: 133 us -> 209 us
    while x22, waiting for transfers between devices: 577 us -> 242 us
    all_gather x11 -> x0, blocking collectives: 216 us -> none  [backward_tick(): shard_piece = lax.all_gather(hidden, 'chan', axis=2, tiled=True)]
    all_to_all x0 -> x11, waiting for transfers between devices: none -> 178 us  [backward_tick(): lax.all_to_all(jnp.stack([hidden] * lax.axis_size('chan')), 'chan', 0, 0)]
    all_to_all x0 -> x11, starting transfers between devices: none -> 75.6 us  [backward_tick(): lax.all_to_all(jnp.stack([hidden] * lax.axis_size('chan')), 'chan', 0, 0)]
    ppermute x22, waiting for transfers between devices: 60.2 us -> 84.7 us  [shifted(): return lax.ppermute(shard, axis, pairs)]
    while x154 -> x308, local copies, waits for them, and re-layouts: 49.4 us -> 34.5 us
    cond x104 -> x120, local copies, waits for them, and re-layouts: 50.2 us -> 49.9 us
  transfers between devices with their start and end apart: 34 -> 45, of which waited for: 23 -> 36; matrix products, arithmetic and copies ran while one was open for 13% -> 17% of each run, Pallas kernels for 0% -> 0%
where the time goes in v1:
time: 1320 us
  waiting for transfers between devices  557 us (42%)
  starting transfers between devices  209 us (16%)
  local copies, waits for them, and re-layouts  191 us (14%)
  blocking collectives  172 us (13%)
  other arithmetic  131 us (10%)
  matrix products  39.6 us (3%)
  between operations  15.3 us (1%)
    while x22, waiting for transfers between devices  242 us
    all_to_all x11, waiting for transfers between devices, backward_tick(): lax.all_to_all(jnp.stack([hidden] * lax.axis_size('chan')), 'chan', 0, 0)  178 us
    all_gather x11, blocking collectives, forward_tick(): shard_piece = lax.all_gather(hidden, 'chan', axis=2, tiled=True)  165 us
    ppermute x22, starting transfers between devices, shifted(): return lax.ppermute(shard, axis, pairs)  133 us
    ppermute x22, waiting for transfers between devices, shifted(): return lax.ppermute(shard, axis, pairs)  84.7 us
    all_to_all x11, starting transfers between devices, backward_tick(): lax.all_to_all(jnp.stack([hidden] * lax.axis_size('chan')), 'chan', 0, 0)  75.6 us
    add x11, other arithmetic, backward_tick(): grad_weight + lax.cond(active, lambda: jnp.einsum('trc,ro->tco', shifted_...  69.3 us
    psum x1, waiting for transfers between devices, local(): lax.psum(backward_state[1].astype(jnp.bfloat16), 'dp').astype(jnp.float32)  52.7 us
  transfers between devices with their start and end apart: 45, of which 36 were waited for; matrix products, arithmetic and copies ran while one was open for 17% of the time, Pallas kernels for 0%

profile of v1, /device:TPU:1, one launch (start us, length us, event | category | flops | bytes accessed | tf_op | source)
XLA Modules:
  0.0 1319.4 jit_solution(3413243918233360718)
XLA Ops:
  8.2 388.7 %while.47 = (s32[]{:T(128)}, bf16[4,1,256,128]{3,2,1,0:T(8,128)(2,1)S(1)}, bf16[4,1,256,128]{3,2,1,0:T(8,128)(2,1)S(1)}, f32[4,1,4]{2,1,0:T(1,128)S(1)}, f32[4,1...) while((s32[]{:T(128)}, ...), condition=%wide.region_7.8_spmd, body=%wide.region_0.7_spmd.sunk | while | flops 604864512 | bytes 33960956 | solution.py:127
  10.7 16.7 %all_gather.12 = bf16[1,256,1024]{2,1,0:T(8,128)(2,1)S(1)} all-gather(bf16[1,256,128]{2,1,0:T(8,128)(2,1)S(1)} %fusion.77), channel_id=1, replica_groups=mesh['dp'=4,'segment'=8,'chan'=8] {'chan'}, dimensions={2}, use_global_device_ids=true | all-gather | bytes 589824 | tf_op jit(solution)/shard_map/while/body/eval_jaxpr/all_gather | solution.py:103
  40.8 14.4 %all_gather.12 = bf16[1,256,1024]{2,1,0:T(8,128)(2,1)S(1)} all-gather(bf16[1,256,128]{2,1,0:T(8,128)(2,1)S(1)} %fusion.77), channel_id=1, replica_groups=mesh['dp'=4,'segment'=8,'chan'=8] {'chan'}, dimensions={2}, use_global_device_ids=true | all-gather | bytes 589824 | tf_op jit(solution)/shard_map/while/body/eval_jaxpr/all_gather | solution.py:103
  71.2 14.9 %all_gather.12 = bf16[1,256,1024]{2,1,0:T(8,128)(2,1)S(1)} all-gather(bf16[1,256,128]{2,1,0:T(8,128)(2,1)S(1)} %fusion.77), channel_id=1, replica_groups=mesh['dp'=4,'segment'=8,'chan'=8] {'chan'}, dimensions={2}, use_global_device_ids=true | all-gather | bytes 589824 | tf_op jit(solution)/shard_map/while/body/eval_jaxpr/all_gather | solution.py:103
  102.1 14.9 %all_gather.12 = bf16[1,256,1024]{2,1,0:T(8,128)(2,1)S(1)} all-gather(bf16[1,256,128]{2,1,0:T(8,128)(2,1)S(1)} %fusion.77), channel_id=1, replica_groups=mesh['dp'=4,'segment'=8,'chan'=8] {'chan'}, dimensions={2}, use_global_device_ids=true | all-gather | bytes 589824 | tf_op jit(solution)/shard_map/while/body/eval_jaxpr/all_gather | solution.py:103
  132.9 14.9 %all_gather.12 = bf16[1,256,1024]{2,1,0:T(8,128)(2,1)S(1)} all-gather(bf16[1,256,128]{2,1,0:T(8,128)(2,1)S(1)} %fusion.77), channel_id=1, replica_groups=mesh['dp'=4,'segment'=8,'chan'=8] {'chan'}, dimensions={2}, use_global_device_ids=true | all-gather | bytes 589824 | tf_op jit(solution)/shard_map/while/body/eval_jaxpr/all_gather | solution.py:103
  147.9 13.5 %collective-permute-start = (bf16[4,1,256,128]{3,2,1,0:T(8,128)(2,1)S(1)}, bf16[4,1,256,128]{3,2,1,0:T(8,128)(2,1)S(1)}, u32[]{:S(2)}, u32[]{:S(2)}) collective-permute-start(bf16[4,1,256,128]{3,2,1,0:T(8,128)(2,1)S(1)} %fusion.78), channel_id=1, source_target_pairs={{0,8},{8,16},{16,24},{24,32},{32,40},{40,48},{48,56},{1,9},{9,17},... | collective-permute-start | bytes 786440 | tf_op jit(solution)/shard_map/while/body/eval_jaxpr/ppermute | solution.py:14
  169.4 14.9 %all_gather.12 = bf16[1,256,1024]{2,1,0:T(8,128)(2,1)S(1)} all-gather(bf16[1,256,128]{2,1,0:T(8,128)(2,1)S(1)} %fusion.77), channel_id=1, replica_groups=mesh['dp'=4,'segment'=8,'chan'=8] {'chan'}, dimensions={2}, use_global_device_ids=true | all-gather | bytes 589824 | tf_op jit(solution)/shard_map/while/body/eval_jaxpr/all_gather | solution.py:103
  184.4 14.2 %collective-permute-start = (bf16[4,1,256,128]{3,2,1,0:T(8,128)(2,1)S(1)}, bf16[4,1,256,128]{3,2,1,0:T(8,128)(2,1)S(1)}, u32[]{:S(2)}, u32[]{:S(2)}) collective-permute-start(bf16[4,1,256,128]{3,2,1,0:T(8,128)(2,1)S(1)} %fusion.78), channel_id=1, source_target_pairs={{0,8},{8,16},{16,24},{24,32},{32,40},{40,48},{48,56},{1,9},{9,17},... | collective-permute-start | bytes 786440 | tf_op jit(solution)/shard_map/while/body/eval_jaxpr/ppermute | solution.py:14
  206.6 14.9 %all_gather.12 = bf16[1,256,1024]{2,1,0:T(8,128)(2,1)S(1)} all-gather(bf16[1,256,128]{2,1,0:T(8,128)(2,1)S(1)} %fusion.77), channel_id=1, replica_groups=mesh['dp'=4,'segment'=8,'chan'=8] {'chan'}, dimensions={2}, use_global_device_ids=true | all-gather | bytes 589824 | tf_op jit(solution)/shard_map/while/body/eval_jaxpr/all_gather | solution.py:103
  221.5 14.1 %collective-permute-start = (bf16[4,1,256,128]{3,2,1,0:T(8,128)(2,1)S(1)}, bf16[4,1,256,128]{3,2,1,0:T(8,128)(2,1)S(1)}, u32[]{:S(2)}, u32[]{:S(2)}) collective-permute-start(bf16[4,1,256,128]{3,2,1,0:T(8,128)(2,1)S(1)} %fusion.78), channel_id=1, source_target_pairs={{0,8},{8,16},{16,24},{24,32},{32,40},{40,48},{48,56},{1,9},{9,17},... | collective-permute-start | bytes 786440 | tf_op jit(solution)/shard_map/while/body/eval_jaxpr/ppermute | solution.py:14
  243.7 14.9 %all_gather.12 = bf16[1,256,1024]{2,1,0:T(8,128)(2,1)S(1)} all-gather(bf16[1,256,128]{2,1,0:T(8,128)(2,1)S(1)} %fusion.77), channel_id=1, replica_groups=mesh['dp'=4,'segment'=8,'chan'=8] {'chan'}, dimensions={2}, use_global_device_ids=true | all-gather | bytes 589824 | tf_op jit(solution)/shard_map/while/body/eval_jaxpr/all_gather | solution.py:103
  258.6 14.1 %collective-permute-start = (bf16[4,1,256,128]{3,2,1,0:T(8,128)(2,1)S(1)}, bf16[4,1,256,128]{3,2,1,0:T(8,128)(2,1)S(1)}, u32[]{:S(2)}, u32[]{:S(2)}) collective-permute-start(bf16[4,1,256,128]{3,2,1,0:T(8,128)(2,1)S(1)} %fusion.78), channel_id=1, source_target_pairs={{0,8},{8,16},{16,24},{24,32},{32,40},{40,48},{48,56},{1,9},{9,17},... | collective-permute-start | bytes 786440 | tf_op jit(solution)/shard_map/while/body/eval_jaxpr/ppermute | solution.py:14
  280.8 14.9 %all_gather.12 = bf16[1,256,1024]{2,1,0:T(8,128)(2,1)S(1)} all-gather(bf16[1,256,128]{2,1,0:T(8,128)(2,1)S(1)} %fusion.77), channel_id=1, replica_groups=mesh['dp'=4,'segment'=8,'chan'=8] {'chan'}, dimensions={2}, use_global_device_ids=true | all-gather | bytes 589824 | tf_op jit(solution)/shard_map/while/body/eval_jaxpr/all_gather | solution.py:103
  295.7 17.8 %collective-permute-start = (bf16[4,1,256,128]{3,2,1,0:T(8,128)(2,1)S(1)}, bf16[4,1,256,128]{3,2,1,0:T(8,128)(2,1)S(1)}, u32[]{:S(2)}, u32[]{:S(2)}) collective-permute-start(bf16[4,1,256,128]{3,2,1,0:T(8,128)(2,1)S(1)} %fusion.78), channel_id=1, source_target_pairs={{0,8},{8,16},{16,24},{24,32},{32,40},{40,48},{48,56},{1,9},{9,17},... | collective-permute-start | bytes 786440 | tf_op jit(solution)/shard_map/while/body/eval_jaxpr/ppermute | solution.py:14
  321.6 14.9 %all_gather.12 = bf16[1,256,1024]{2,1,0:T(8,128)(2,1)S(1)} all-gather(bf16[1,256,128]{2,1,0:T(8,128)(2,1)S(1)} %fusion.77), channel_id=1, replica_groups=mesh['dp'=4,'segment'=8,'chan'=8] {'chan'}, dimensions={2}, use_global_device_ids=true | all-gather | bytes 589824 | tf_op jit(solution)/shard_map/while/body/eval_jaxpr/all_gather | solution.py:103
  336.5 14.1 %collective-permute-start = (bf16[4,1,256,128]{3,2,1,0:T(8,128)(2,1)S(1)}, bf16[4,1,256,128]{3,2,1,0:T(8,128)(2,1)S(1)}, u32[]{:S(2)}, u32[]{:S(2)}) collective-permute-start(bf16[4,1,256,128]{3,2,1,0:T(8,128)(2,1)S(1)} %fusion.78), channel_id=1, source_target_pairs={{0,8},{8,16},{16,24},{24,32},{32,40},{40,48},{48,56},{1,9},{9,17},... | collective-permute-start | bytes 786440 | tf_op jit(solution)/shard_map/while/body/eval_jaxpr/ppermute | solution.py:14
  358.6 14.9 %all_gather.12 = bf16[1,256,1024]{2,1,0:T(8,128)(2,1)S(1)} all-gather(bf16[1,256,128]{2,1,0:T(8,128)(2,1)S(1)} %fusion.77), channel_id=1, replica_groups=mesh['dp'=4,'segment'=8,'chan'=8] {'chan'}, dimensions={2}, use_global_device_ids=true | all-gather | bytes 589824 | tf_op jit(solution)/shard_map/while/body/eval_jaxpr/all_gather | solution.py:103
  373.6 17.8 %collective-permute-start = (bf16[4,1,256,128]{3,2,1,0:T(8,128)(2,1)S(1)}, bf16[4,1,256,128]{3,2,1,0:T(8,128)(2,1)S(1)}, u32[]{:S(2)}, u32[]{:S(2)}) collective-permute-start(bf16[4,1,256,128]{3,2,1,0:T(8,128)(2,1)S(1)} %fusion.78), channel_id=1, source_target_pairs={{0,8},{8,16},{16,24},{24,32},{32,40},{40,48},{48,56},{1,9},{9,17},... | collective-permute-start | bytes 786440 | tf_op jit(solution)/shard_map/while/body/eval_jaxpr/ppermute | solution.py:14
  397.0 845.7 %while.48 = (s32[]{:T(128)}, bf16[4,1,256,128]{3,2,1,0:T(8,128)(2,1)S(1)}, f32[9,1024,128]{2,1,0:T(8,128)}, f32[128]{0:T(128)}, f32[128]{0:T(128)}, /*index=5*/p...) while((s32[]{:T(128)}, ...), condition=%wide.region_20.21_spmd.clone, body=%wide.region_8.20_spmd.clone.sunk | while | flops 1211990528 | bytes 65440856 | solution.py:210
  406.1 14.4 %all-to-all-done = bf16[8,1,256,128]{3,2,1,0:T(8,128)(2,1)S(1)} async-done(((bf16[8,1,256,128]{3,2,1,0:T(8,128)(2,1)}), bf16[8,1,256,128]{3,2,1,0:T(8,128)(2,1)S(1)}, u32[]{:S(2)}, u32[]{:S(2)}) %all-to-all-start) | async-done | bytes 524320 | tf_op jit(solution)/shard_map/while/body/eval_jaxpr/all_to_all | solution.py:159
  423.1 46.8 %reduce-scatter.6.cloned.1.call-done = bf16[128,256]{1,0:T(8,128)(2,1)} async-done(((bf16[1024,256]{1,0:T(8,128)(2,1)}), bf16[128,256]{1,0:T(8,128)(2,1)}) %reduce-scatter.6.cloned.1.call-update) | async-done | bytes 65552 | tf_op jit(solution)/shard_map/while
  484.6 8.5 all-to-all-start
  493.1 14.4 %all-to-all-done = bf16[8,1,256,128]{3,2,1,0:T(8,128)(2,1)S(1)} async-done(((bf16[8,1,256,128]{3,2,1,0:T(8,128)(2,1)}), bf16[8,1,256,128]{3,2,1,0:T(8,128)(2,1)S(1)}, u32[]{:S(2)}, u32[]{:S(2)}) %all-to-all-start) | async-done | bytes 524320 | tf_op jit(solution)/shard_map/while/body/eval_jaxpr/all_to_all | solution.py:159
  510.0 17.9 %reduce-scatter.6.cloned.1.call-done = bf16[128,256]{1,0:T(8,128)(2,1)} async-done(((bf16[1024,256]{1,0:T(8,128)(2,1)}), bf16[128,256]{1,0:T(8,128)(2,1)}) %reduce-scatter.6.cloned.1.call-update) | async-done | bytes 65552 | tf_op jit(solution)/shard_map/while
  543.6 7.7 all-to-all-start
  551.3 14.4 %all-to-all-done = bf16[8,1,256,128]{3,2,1,0:T(8,128)(2,1)S(1)} async-done(((bf16[8,1,256,128]{3,2,1,0:T(8,128)(2,1)}), bf16[8,1,256,128]{3,2,1,0:T(8,128)(2,1)S(1)}, u32[]{:S(2)}, u32[]{:S(2)}) %all-to-all-start) | async-done | bytes 524320 | tf_op jit(solution)/shard_map/while/body/eval_jaxpr/all_to_all | solution.py:159
  568.2 26.9 %reduce-scatter.6.cloned.1.call-done = bf16[128,256]{1,0:T(8,128)(2,1)} async-done(((bf16[1024,256]{1,0:T(8,128)(2,1)}), bf16[128,256]{1,0:T(8,128)(2,1)}) %reduce-scatter.6.cloned.1.call-update) | async-done | bytes 65552 | tf_op jit(solution)/shard_map/while
  618.4 14.4 %all-to-all-done = bf16[8,1,256,128]{3,2,1,0:T(8,128)(2,1)S(1)} async-done(((bf16[8,1,256,128]{3,2,1,0:T(8,128)(2,1)}), bf16[8,1,256,128]{3,2,1,0:T(8,128)(2,1)S(1)}, u32[]{:S(2)}, u32[]{:S(2)}) %all-to-all-start) | async-done | bytes 524320 | tf_op jit(solution)/shard_map/while/body/eval_jaxpr/all_to_all | solution.py:159
  635.3 32.5 %reduce-scatter.6.cloned.1.call-done = bf16[128,256]{1,0:T(8,128)(2,1)} async-done(((bf16[1024,256]{1,0:T(8,128)(2,1)}), bf16[128,256]{1,0:T(8,128)(2,1)}) %reduce-scatter.6.cloned.1.call-update) | async-done | bytes 65552 | tf_op jit(solution)/shard_map/while
  690.7 20.0 %all-to-all-done = bf16[8,1,256,128]{3,2,1,0:T(8,128)(2,1)S(1)} async-done(((bf16[8,1,256,128]{3,2,1,0:T(8,128)(2,1)}), bf16[8,1,256,128]{3,2,1,0:T(8,128)(2,1)S(1)}, u32[]{:S(2)}, u32[]{:S(2)}) %all-to-all-start) | async-done | bytes 524320 | tf_op jit(solution)/shard_map/while/body/eval_jaxpr/all_to_all | solution.py:159
  713.2 29.2 %reduce-scatter.6.cloned.1.call-done = bf16[128,256]{1,0:T(8,128)(2,1)} async-done(((bf16[1024,256]{1,0:T(8,128)(2,1)}), bf16[128,256]{1,0:T(8,128)(2,1)}) %reduce-scatter.6.cloned.1.call-update) | async-done | bytes 65552 | tf_op jit(solution)/shard_map/while
  765.6 17.2 %all-to-all-done = bf16[8,1,256,128]{3,2,1,0:T(8,128)(2,1)S(1)} async-done(((bf16[8,1,256,128]{3,2,1,0:T(8,128)(2,1)}), bf16[8,1,256,128]{3,2,1,0:T(8,128)(2,1)S(1)}, u32[]{:S(2)}, u32[]{:S(2)}) %all-to-all-start) | async-done | bytes 524320 | tf_op jit(solution)/shard_map/while/body/eval_jaxpr/all_to_all | solution.py:159
  785.3 38.9 %reduce-scatter.6.cloned.1.call-done = bf16[128,256]{1,0:T(8,128)(2,1)} async-done(((bf16[1024,256]{1,0:T(8,128)(2,1)}), bf16[128,256]{1,0:T(8,128)(2,1)}) %reduce-scatter.6.cloned.1.call-update) | async-done | bytes 65552 | tf_op jit(solution)/shard_map/while
  839.8 7.7 all-to-all-start
  847.5 17.2 %all-to-all-done = bf16[8,1,256,128]{3,2,1,0:T(8,128)(2,1)S(1)} async-done(((bf16[8,1,256,128]{3,2,1,0:T(8,128)(2,1)}), bf16[8,1,256,128]{3,2,1,0:T(8,128)(2,1)S(1)}, u32[]{:S(2)}, u32[]{:S(2)}) %all-to-all-start) | async-done | bytes 524320 | tf_op jit(solution)/shard_map/while/body/eval_jaxpr/all_to_all | solution.py:159
  867.2 38.9 %reduce-scatter.6.cloned.1.call-done = bf16[128,256]{1,0:T(8,128)(2,1)} async-done(((bf16[1024,256]{1,0:T(8,128)(2,1)}), bf16[128,256]{1,0:T(8,128)(2,1)}) %reduce-scatter.6.cloned.1.call-update) | async-done | bytes 65552 | tf_op jit(solution)/shard_map/while
  931.9 17.2 %all-to-all-done = bf16[8,1,256,128]{3,2,1,0:T(8,128)(2,1)S(1)} async-done(((bf16[8,1,256,128]{3,2,1,0:T(8,128)(2,1)}), bf16[8,1,256,128]{3,2,1,0:T(8,128)(2,1)S(1)}, u32[]{:S(2)}, u32[]{:S(2)}) %all-to-all-start) | async-done | bytes 524320 | tf_op jit(solution)/shard_map/while/body/eval_jaxpr/all_to_all | solution.py:159
  949.1 32.1 %conditional.10 = (f32[9,1024,128]{2,1,0:T(8,128)}) conditional(s32[]{:T(128)} %convert_element_type.705, () %tuple.160, (bf16[1,256,8,128]{3,1,0,2:T(8,128)(2,1)S(1)}, pred[]{:T(512)}, pred[]{:T(512)}, bf16[1,1,256,128]{3,2,1,0:T(8,128)(2,1)}, bf16[1,1,256,128]{3,2,1,0:T(8,128)(2,1)S(1)}, /*index=5*/bf16[1,1,256,128]{3,2,1,0:T(8,128)(2,1)}) %tuple.178), branch_computations={%region_16.16_spmd, %region_17.17_spmd} | conditional | flops 604045312 | bytes 35848256 | solution.py:161
  1006.3 7.7 all-to-all-start
  1014.0 17.2 %all-to-all-done = bf16[8,1,256,128]{3,2,1,0:T(8,128)(2,1)S(1)} async-done(((bf16[8,1,256,128]{3,2,1,0:T(8,128)(2,1)}), bf16[8,1,256,128]{3,2,1,0:T(8,128)(2,1)S(1)}, u32[]{:S(2)}, u32[]{:S(2)}) %all-to-all-start) | async-done | bytes 524320 | tf_op jit(solution)/shard_map/while/body/eval_jaxpr/all_to_all | solution.py:159
  1031.2 32.1 %conditional.10 = (f32[9,1024,128]{2,1,0:T(8,128)}) conditional(s32[]{:T(128)} %convert_element_type.705, () %tuple.160, (bf16[1,256,8,128]{3,1,0,2:T(8,128)(2,1)S(1)}, pred[]{:T(512)}, pred[]{:T(512)}, bf16[1,1,256,128]{3,2,1,0:T(8,128)(2,1)}, bf16[1,1,256,128]{3,2,1,0:T(8,128)(2,1)S(1)}, /*index=5*/bf16[1,1,256,128]{3,2,1,0:T(8,128)(2,1)}) %tuple.178), branch_computations={%region_16.16_spmd, %region_17.17_spmd} | conditional | flops 604045312 | bytes 35848256 | solution.py:161
  1094.6 14.4 %all-to-all-done = bf16[8,1,256,128]{3,2,1,0:T(8,128)(2,1)S(1)} async-done(((bf16[8,1,256,128]{3,2,1,0:T(8,128)(2,1)}), bf16[8,1,256,128]{3,2,1,0:T(8,128)(2,1)S(1)}, u32[]{:S(2)}, u32[]{:S(2)}) %all-to-all-start) | async-done | bytes 524320 | tf_op jit(solution)/shard_map/while/body/eval_jaxpr/all_to_all | solution.py:159
  1109.0 32.1 %conditional.10 = (f32[9,1024,128]{2,1,0:T(8,128)}) conditional(s32[]{:T(128)} %convert_element_type.705, () %tuple.160, (bf16[1,256,8,128]{3,1,0,2:T(8,128)(2,1)S(1)}, pred[]{:T(512)}, pred[]{:T(512)}, bf16[1,1,256,128]{3,2,1,0:T(8,128)(2,1)}, bf16[1,1,256,128]{3,2,1,0:T(8,128)(2,1)S(1)}, /*index=5*/bf16[1,1,256,128]{3,2,1,0:T(8,128)(2,1)}) %tuple.178), branch_computations={%region_16.16_spmd, %region_17.17_spmd} | conditional | flops 604045312 | bytes 35848256 | solution.py:161
  1151.5 17.7 %collective-permute-done.1 = bf16[4,1,256,128]{3,2,1,0:T(8,128)(2,1)S(1)} collective-permute-done((bf16[4,1,256,128]{3,2,1,0:T(8,128)(2,1)}, bf16[4,1,256,128]{3,2,1,0:T(8,128)(2,1)S(1)}, u32[]{:S(2)}, u32[]{:S(2)}) %collective-permute-start.1) | collective-permute-done | bytes 262176 | tf_op jit(solution)/shard_map/while/body/eval_jaxpr/ppermute | solution.py:14
  1181.4 17.4 %all-to-all-done = bf16[8,1,256,128]{3,2,1,0:T(8,128)(2,1)S(1)} async-done(((bf16[8,1,256,128]{3,2,1,0:T(8,128)(2,1)}), bf16[8,1,256,128]{3,2,1,0:T(8,128)(2,1)S(1)}, u32[]{:S(2)}, u32[]{:S(2)}) %all-to-all-start) | async-done | bytes 524320 | tf_op jit(solution)/shard_map/while/body/eval_jaxpr/all_to_all | solution.py:159
  1198.8 32.1 %conditional.10 = (f32[9,1024,128]{2,1,0:T(8,128)}) conditional(s32[]{:T(128)} %convert_element_type.705, () %tuple.160, (bf16[1,256,8,128]{3,1,0,2:T(8,128)(2,1)S(1)}, pred[]{:T(512)}, pred[]{:T(512)}, bf16[1,1,256,128]{3,2,1,0:T(8,128)(2,1)}, bf16[1,1,256,128]{3,2,1,0:T(8,128)(2,1)S(1)}, /*index=5*/bf16[1,1,256,128]{3,2,1,0:T(8,128)(2,1)}) %tuple.178), branch_computations={%region_16.16_spmd, %region_17.17_spmd} | conditional | flops 604045312 | bytes 35848256 | solution.py:161
  1255.4 52.7 %all-reduce.6.cloned.1.call-done = bf16[1,9,1024,128]{3,2,1,0:T(8,128)(2,1)} async-done(((bf16[1,9,1024,128]{3,2,1,0:T(8,128)(2,1)}), bf16[1,9,1024,128]{3,2,1,0:T(8,128)(2,1)}) %all-reduce.6.cloned.1.call-update) | async-done | bytes 2359312 | tf_op jit(solution)/shard_map/psum | solution.py:212
  (1076 shorter events, 563.0 us)
Async XLA Ops:
  31.2 7.1 collective-permute-start
  59.1 9.6 collective-permute-start
  89.9 9.6 collective-permute-start
  120.7 9.6 collective-permute-start
  147.9 19.0 %collective-permute-start = (bf16[4,1,256,128]{3,2,1,0:T(8,128)(2,1)S(1)}, bf16[4,1,256,128]{3,2,1,0:T(8,128)(2,1)S(1)}, u32[]{:S(2)}, u32[]{:S(2)}) collective-permute-start(bf16[4,1,256,128]{3,2,1,0:T(8,128)(2,1)S(1)} %fusion.78), channel_id=1, source_target_pairs={{0,8},{8,16},{16,24},{24,32},{32,40},{40,48},{48,56},{1,9},{9,17},... | collective-permute-start | bytes 786440 | tf_op jit(solution)/shard_map/while/body/eval_jaxpr/ppermute | solution.py:14
  184.4 19.7 %collective-permute-start = (bf16[4,1,256,128]{3,2,1,0:T(8,128)(2,1)S(1)}, bf16[4,1,256,128]{3,2,1,0:T(8,128)(2,1)S(1)}, u32[]{:S(2)}, u32[]{:S(2)}) collective-permute-start(bf16[4,1,256,128]{3,2,1,0:T(8,128)(2,1)S(1)} %fusion.78), channel_id=1, source_target_pairs={{0,8},{8,16},{16,24},{24,32},{32,40},{40,48},{48,56},{1,9},{9,17},... | collective-permute-start | bytes 786440 | tf_op jit(solution)/shard_map/while/body/eval_jaxpr/ppermute | solution.py:14
  221.5 19.6 %collective-permute-start = (bf16[4,1,256,128]{3,2,1,0:T(8,128)(2,1)S(1)}, bf16[4,1,256,128]{3,2,1,0:T(8,128)(2,1)S(1)}, u32[]{:S(2)}, u32[]{:S(2)}) collective-permute-start(bf16[4,1,256,128]{3,2,1,0:T(8,128)(2,1)S(1)} %fusion.78), channel_id=1, source_target_pairs={{0,8},{8,16},{16,24},{24,32},{32,40},{40,48},{48,56},{1,9},{9,17},... | collective-permute-start | bytes 786440 | tf_op jit(solution)/shard_map/while/body/eval_jaxpr/ppermute | solution.py:14
  258.6 19.6 %collective-permute-start = (bf16[4,1,256,128]{3,2,1,0:T(8,128)(2,1)S(1)}, bf16[4,1,256,128]{3,2,1,0:T(8,128)(2,1)S(1)}, u32[]{:S(2)}, u32[]{:S(2)}) collective-permute-start(bf16[4,1,256,128]{3,2,1,0:T(8,128)(2,1)S(1)} %fusion.78), channel_id=1, source_target_pairs={{0,8},{8,16},{16,24},{24,32},{32,40},{40,48},{48,56},{1,9},{9,17},... | collective-permute-start | bytes 786440 | tf_op jit(solution)/shard_map/while/body/eval_jaxpr/ppermute | solution.py:14
  295.7 23.3 %collective-permute-start = (bf16[4,1,256,128]{3,2,1,0:T(8,128)(2,1)S(1)}, bf16[4,1,256,128]{3,2,1,0:T(8,128)(2,1)S(1)}, u32[]{:S(2)}, u32[]{:S(2)}) collective-permute-start(bf16[4,1,256,128]{3,2,1,0:T(8,128)(2,1)S(1)} %fusion.78), channel_id=1, source_target_pairs={{0,8},{8,16},{16,24},{24,32},{32,40},{40,48},{48,56},{1,9},{9,17},... | collective-permute-start | bytes 786440 | tf_op jit(solution)/shard_map/while/body/eval_jaxpr/ppermute | solution.py:14
  336.5 19.6 %collective-permute-start = (bf16[4,1,256,128]{3,2,1,0:T(8,128)(2,1)S(1)}, bf16[4,1,256,128]{3,2,1,0:T(8,128)(2,1)S(1)}, u32[]{:S(2)}, u32[]{:S(2)}) collective-permute-start(bf16[4,1,256,128]{3,2,1,0:T(8,128)(2,1)S(1)} %fusion.78), channel_id=1, source_target_pairs={{0,8},{8,16},{16,24},{24,32},{32,40},{40,48},{48,56},{1,9},{9,17},... | collective-permute-start | bytes 786440 | tf_op jit(solution)/shard_map/while/body/eval_jaxpr/ppermute | solution.py:14
  373.6 23.3 %collective-permute-start = (bf16[4,1,256,128]{3,2,1,0:T(8,128)(2,1)S(1)}, bf16[4,1,256,128]{3,2,1,0:T(8,128)(2,1)S(1)}, u32[]{:S(2)}, u32[]{:S(2)}) collective-permute-start(bf16[4,1,256,128]{3,2,1,0:T(8,128)(2,1)S(1)} %fusion.78), channel_id=1, source_target_pairs={{0,8},{8,16},{16,24},{24,32},{32,40},{40,48},{48,56},{1,9},{9,17},... | collective-permute-start | bytes 786440 | tf_op jit(solution)/shard_map/while/body/eval_jaxpr/ppermute | solution.py:14
  397.0 72.9 %reduce-scatter.6.cloned.1.call-start = ((), (), s32[]{:S(2)}) async-start(), calls=%async_computation.3 | async-start | bytes 589824 | tf_op jit(solution)/shard_map/while
  401.7 18.8 %all-to-all-start = ((bf16[8,1,256,128]{3,2,1,0:T(8,128)(2,1)}), bf16[8,1,256,128]{3,2,1,0:T(8,128)(2,1)S(1)}, u32[]{:S(2)}, u32[]{:S(2)}) async-start(bf16[8,1,256,128]{3,2,1,0:T(8,128)(2,1)} %stack.29), calls=%async_computation.1 | async-start | bytes 1048576 | tf_op jit(solution)/shard_map/while/body/eval_jaxpr/all_to_all | solution.py:159
  472.5 7.3 collective-permute-start.1
  479.9 48.1 %reduce-scatter.6.cloned.1.call-start = ((), (), s32[]{:S(2)}) async-start(), calls=%async_computation.3 | async-start | bytes 589824 | tf_op jit(solution)/shard_map/while
  484.6 22.9 %all-to-all-start = ((bf16[8,1,256,128]{3,2,1,0:T(8,128)(2,1)}), bf16[8,1,256,128]{3,2,1,0:T(8,128)(2,1)S(1)}, u32[]{:S(2)}, u32[]{:S(2)}) async-start(bf16[8,1,256,128]{3,2,1,0:T(8,128)(2,1)} %stack.29), calls=%async_computation.1 | async-start | bytes 1048576 | tf_op jit(solution)/shard_map/while/body/eval_jaxpr/all_to_all | solution.py:159
  530.5 7.8 collective-permute-start.1
  538.9 56.2 %reduce-scatter.6.cloned.1.call-start = ((), (), s32[]{:S(2)}) async-start(), calls=%async_computation.3 | async-start | bytes 589824 | tf_op jit(solution)/shard_map/while
  543.6 22.1 %all-to-all-start = ((bf16[8,1,256,128]{3,2,1,0:T(8,128)(2,1)}), bf16[8,1,256,128]{3,2,1,0:T(8,128)(2,1)S(1)}, u32[]{:S(2)}, u32[]{:S(2)}) async-start(bf16[8,1,256,128]{3,2,1,0:T(8,128)(2,1)} %stack.29), calls=%async_computation.1 | async-start | bytes 1048576 | tf_op jit(solution)/shard_map/while/body/eval_jaxpr/all_to_all | solution.py:159
  597.7 7.8 collective-permute-start.1
  606.0 61.8 %reduce-scatter.6.cloned.1.call-start = ((), (), s32[]{:S(2)}) async-start(), calls=%async_computation.3 | async-start | bytes 589824 | tf_op jit(solution)/shard_map/while
  610.7 22.0 %all-to-all-start = ((bf16[8,1,256,128]{3,2,1,0:T(8,128)(2,1)}), bf16[8,1,256,128]{3,2,1,0:T(8,128)(2,1)S(1)}, u32[]{:S(2)}, u32[]{:S(2)}) async-start(bf16[8,1,256,128]{3,2,1,0:T(8,128)(2,1)} %stack.29), calls=%async_computation.1 | async-start | bytes 1048576 | tf_op jit(solution)/shard_map/while/body/eval_jaxpr/all_to_all | solution.py:159
  670.4 7.8 collective-permute-start.1
  678.7 63.8 %reduce-scatter.6.cloned.1.call-start = ((), (), s32[]{:S(2)}) async-start(), calls=%async_computation.3 | async-start | bytes 589824 | tf_op jit(solution)/shard_map/while
  683.4 27.3 %all-to-all-start = ((bf16[8,1,256,128]{3,2,1,0:T(8,128)(2,1)}), bf16[8,1,256,128]{3,2,1,0:T(8,128)(2,1)S(1)}, u32[]{:S(2)}, u32[]{:S(2)}) async-start(bf16[8,1,256,128]{3,2,1,0:T(8,128)(2,1)} %stack.29), calls=%async_computation.1 | async-start | bytes 1048576 | tf_op jit(solution)/shard_map/while/body/eval_jaxpr/all_to_all | solution.py:159
  745.0 7.8 collective-permute-start.1
  753.4 70.8 %reduce-scatter.6.cloned.1.call-start = ((), (), s32[]{:S(2)}) async-start(), calls=%async_computation.3 | async-start | bytes 589824 | tf_op jit(solution)/shard_map/while
  758.1 24.6 %all-to-all-start = ((bf16[8,1,256,128]{3,2,1,0:T(8,128)(2,1)}), bf16[8,1,256,128]{3,2,1,0:T(8,128)(2,1)S(1)}, u32[]{:S(2)}, u32[]{:S(2)}) async-start(bf16[8,1,256,128]{3,2,1,0:T(8,128)(2,1)} %stack.29), calls=%async_computation.1 | async-start | bytes 1048576 | tf_op jit(solution)/shard_map/while/body/eval_jaxpr/all_to_all | solution.py:159
  826.8 7.8 collective-permute-start.1
  835.1 71.0 %reduce-scatter.6.cloned.1.call-start = ((), (), s32[]{:S(2)}) async-start(), calls=%async_computation.3 | async-start | bytes 589824 | tf_op jit(solution)/shard_map/while
  839.8 24.9 %all-to-all-start = ((bf16[8,1,256,128]{3,2,1,0:T(8,128)(2,1)}), bf16[8,1,256,128]{3,2,1,0:T(8,128)(2,1)S(1)}, u32[]{:S(2)}, u32[]{:S(2)}) async-start(bf16[8,1,256,128]{3,2,1,0:T(8,128)(2,1)} %stack.29), calls=%async_computation.1 | async-start | bytes 1048576 | tf_op jit(solution)/shard_map/while/body/eval_jaxpr/all_to_all | solution.py:159
  908.7 7.8 collective-permute-start.1
  917.1 70.9 %reduce-scatter.6.cloned.1.call-start = ((), (), s32[]{:S(2)}) async-start(), calls=%async_computation.3 | async-start | bytes 589824 | tf_op jit(solution)/shard_map/while
  924.5 24.6 %all-to-all-start = ((bf16[8,1,256,128]{3,2,1,0:T(8,128)(2,1)}), bf16[8,1,256,128]{3,2,1,0:T(8,128)(2,1)S(1)}, u32[]{:S(2)}, u32[]{:S(2)}) async-start(bf16[8,1,256,128]{3,2,1,0:T(8,128)(2,1)} %stack.29), calls=%async_computation.1 | async-start | bytes 1048576 | tf_op jit(solution)/shard_map/while/body/eval_jaxpr/all_to_all | solution.py:159
  990.5 7.8 collective-permute-start.1
  998.9 68.2 %reduce-scatter.6.cloned.1.call-start = ((), (), s32[]{:S(2)}) async-start(), calls=%async_computation.3 | async-start | bytes 589824 | tf_op jit(solution)/shard_map/while
  1006.3 24.9 %all-to-all-start = ((bf16[8,1,256,128]{3,2,1,0:T(8,128)(2,1)}), bf16[8,1,256,128]{3,2,1,0:T(8,128)(2,1)S(1)}, u32[]{:S(2)}, u32[]{:S(2)}) async-start(bf16[8,1,256,128]{3,2,1,0:T(8,128)(2,1)} %stack.29), calls=%async_computation.1 | async-start | bytes 1048576 | tf_op jit(solution)/shard_map/while/body/eval_jaxpr/all_to_all | solution.py:159
  1069.7 12.5 collective-permute-start.1
  1082.2 58.8 %reduce-scatter.6.cloned.1.call-start = ((), (), s32[]{:S(2)}) async-start(), calls=%async_computation.3 | async-start | bytes 589824 | tf_op jit(solution)/shard_map/while
  1089.7 19.3 %all-to-all-start = ((bf16[8,1,256,128]{3,2,1,0:T(8,128)(2,1)}), bf16[8,1,256,128]{3,2,1,0:T(8,128)(2,1)S(1)}, u32[]{:S(2)}, u32[]{:S(2)}) async-start(bf16[8,1,256,128]{3,2,1,0:T(8,128)(2,1)} %stack.29), calls=%async_computation.1 | async-start | bytes 1048576 | tf_op jit(solution)/shard_map/while/body/eval_jaxpr/all_to_all | solution.py:159
  1143.7 25.5 %collective-permute-start.1 = (bf16[4,1,256,128]{3,2,1,0:T(8,128)(2,1)}, bf16[4,1,256,128]{3,2,1,0:T(8,128)(2,1)S(1)}, u32[]{:S(2)}, u32[]{:S(2)}) collective-permute-start(bf16[4,1,256,128]{3,2,1,0:T(8,128)(2,1)} %fusion.82), channel_id=1, source_target_pairs={{8,0},{16,8},{24,16},{32,24},{40,32},{48,40},{56,48},{9,1},{17,9},... | collective-permute-start | bytes 786440 | tf_op jit(solution)/shard_map/while/body/eval_jaxpr/ppermute | solution.py:14
  1145.0 24.2 %copy-start.13 = (f32[4,1,4]{2,1,0:T(1,128)S(1)}, f32[4,1,4]{2,1,0:T(1,128)}, u32[]{:S(2)}) copy-start(f32[4,1,4]{2,1,0:T(1,128)} %copy-done.12) | copy-start | bytes 196 | tf_op jit(solution)/shard_map/while
  1145.0 24.2 %copy-start.15 = (f32[4,1,4]{2,1,0:T(1,128)S(1)}, f32[4,1,4]{2,1,0:T(1,128)}, u32[]{:S(2)}) copy-start(f32[4,1,4]{2,1,0:T(1,128)} %copy-done.14) | copy-start | bytes 196 | tf_op jit(solution)/shard_map/while
  1151.5 17.7 %copy-start.7 = (f32[128]{0:T(128)}, f32[128]{0:T(128)S(1)}, u32[]{:S(2)}) copy-start(f32[128]{0:T(128)S(1)} %get-tuple-element.1596) | copy-start | bytes 1540 | tf_op jit(solution)/shard_map/while
  1169.3 61.6 %reduce-scatter.6.cloned.1.call-start = ((), (), s32[]{:S(2)}) async-start(), calls=%async_computation.3 | async-start | bytes 589824 | tf_op jit(solution)/shard_map/while
  1176.7 22.1 %all-to-all-start = ((bf16[8,1,256,128]{3,2,1,0:T(8,128)(2,1)}), bf16[8,1,256,128]{3,2,1,0:T(8,128)(2,1)S(1)}, u32[]{:S(2)}, u32[]{:S(2)}) async-start(bf16[8,1,256,128]{3,2,1,0:T(8,128)(2,1)} %stack.29), calls=%async_computation.1 | async-start | bytes 1048576 | tf_op jit(solution)/shard_map/while/body/eval_jaxpr/all_to_all | solution.py:159
  1233.5 9.1 collective-permute-start.1
  1242.6 65.5 %all-reduce.6.cloned.1.call-start = ((), (), s32[]{:S(2)}) async-start(), calls=%async_computation.2 | async-start | bytes 4718592 | tf_op jit(solution)/shard_map/psum | solution.py:212
  (132 other events, 574.3 us)
Sparse Core Ops, SparseCore 0:
  400.6 69.2 reduce-scatter.5
  483.4 44.4 reduce-scatter.5
  542.4 52.5 reduce-scatter.5
  609.5 58.1 reduce-scatter.5
  682.2 60.1 reduce-scatter.5
  756.9 67.2 reduce-scatter.5
  838.7 67.4 reduce-scatter.5
  923.3 64.5 reduce-scatter.5
  1005.2 61.8 reduce-scatter.5
  1088.5 41.5 reduce-scatter.5
  1175.5 27.1 reduce-scatter.5
Sparse Core Ops, SparseCore 1:
  1247.0 61.1 all-reduce.5
